TPU v7x, 256 devices: a whole 4x4x8 slice. The times are simulated.
256 devices in a mesh: seq: 32 (over x, z_lo, core), dp: 8 (over z_hi, y).
Axes of the slice: x: 4, y: 4, z: 8 (z_hi: 2, z_lo: 4; z = z_hi * 4 + z_lo), core: 2. Of those that a mesh axis runs over, the one named last changes fastest.
Arguments:
- tokens: bfloat16 [8, 16384, 1536], P('dp', 'seq'), may hold values from -6 to 6
- cotangent: bfloat16 [8, 16384, 1536], P('dp', 'seq'), may hold values from -6 to 6
- conv_weight: float32 [3, 1536], replicated, may hold values from -3.5 to 3.5
- gate_weight: bfloat16 [1536, 1536], P('seq'), may hold values from -0.15625 to 0.15625
- leading_block_factor: bfloat16 [128, 128, 128], P('seq'), may hold values from -0.5 to 0.5
- trailing_block_factor: bfloat16 [128, 128, 128], P('seq'), may hold values from -0.5 to 0.5
Outputs:
- mixed: bfloat16 [8, 16384, 1536], P('dp', 'seq')
- grad_tokens: bfloat16 [8, 16384, 1536], P('dp', 'seq')
- grad_conv: float32 [3, 1536], replicated
- grad_gate: float32 [1536, 1536], P('seq')
- grad_first: float32 [128, 128, 128], P('seq')
- trailing_factor_gradient: float32 [128, 128, 128], P('seq')
All inputs are finite; a program needn't handle non-finite values.
Results may differ from a plain program's by a relative error of at most 0.0067.
Values may be sent and summed in bfloat16 or wider, within the bound.
No kernel may reach another device: no remote copies, remote signals or barrier semaphores. Data moves between devices by JAX's collectives and lax.ppermute only.
A program may use at most 128 MiB of HBM per device.

v0:
```python
import jax
import jax.numpy as jnp
from jax import lax
from jax.sharding import PartitionSpec as P


def with_halo(array, sides, width):
    for axis, dim in sides:
        count, length = (lax.axis_size(axis), array.shape[dim])
        up = [(i, (i + 1) % count) for i in range(count - 1)]
        down = [(j, i) for i, j in up]
        last = lax.slice_in_dim(array, length - width, length, axis=dim)
        first = lax.slice_in_dim(array, 0, width, axis=dim)
        before = lax.ppermute(last, axis, up)
        after = lax.ppermute(first, axis, down)
        array = jnp.concatenate([before, array, after], axis=dim)
    return array


def extend(values):
    return with_halo(values, (("seq", 0),), 1)


def regroup(values):
    return lax.all_to_all(values, "seq", split_axis=0, concat_axis=1, tiled=True)


def shards(
    tokens, cotangent, conv_weight, gate_weight, leading_block_factor, trailing_block_factor
):
    features = tokens[0]
    grad_out = cotangent[0]
    tok_rows = features.shape[0]
    feat_width = features.shape[1]
    local_blocks = leading_block_factor.shape[0]
    block_size = leading_block_factor.shape[1]
    feat_wide = features.astype(jnp.float32)
    pad_feat = extend(features).astype(jnp.float32)
    conv_in = (
        conv_weight[0] * pad_feat[:-2] + conv_weight[1] * feat_wide + conv_weight[2] * pad_feat[2:]
    ).astype(jnp.bfloat16)
    convolution_block_list = conv_in.reshape(local_blocks, block_size, feat_width)
    leading_output = jnp.einsum(
        "shz,szy->hsy",
        leading_block_factor,
        convolution_block_list,
        preferred_element_type=jnp.float32,
    ).astype(jnp.bfloat16)
    column_layout = regroup(leading_output)
    trailing_output = jnp.einsum(
        "vpn,vnu->pvu", trailing_block_factor, column_layout, preferred_element_type=jnp.float32
    ).astype(jnp.bfloat16)
    monarch = regroup(trailing_output).reshape(tok_rows, feat_width)
    whole_gate = lax.all_gather(gate_weight, "seq", axis=0, tiled=True)
    gate_act = jnp.dot(features, whole_gate, preferred_element_type=jnp.float32)
    mon_wide = monarch.astype(jnp.float32)
    grad_wide = grad_out.astype(jnp.float32)
    mixed = (mon_wide * gate_act).astype(jnp.bfloat16)
    d_monarch = (grad_wide * gate_act).astype(jnp.bfloat16)
    d_gate = (grad_wide * mon_wide).astype(jnp.bfloat16)
    second_factor_delta = lax.all_to_all(
        d_monarch.reshape(local_blocks, block_size, feat_width),
        "seq",
        split_axis=1,
        concat_axis=0,
        tiled=True,
    )
    d_inner = jnp.einsum(
        "ica,cid->aid",
        trailing_block_factor,
        second_factor_delta,
        preferred_element_type=jnp.float32,
    ).astype(jnp.bfloat16)
    trailing_factor_gradient = jnp.einsum(
        "wxn,xon->xwo", second_factor_delta, column_layout, preferred_element_type=jnp.float32
    )
    d_first = regroup(d_inner)
    d_conv = (
        jnp.einsum(
            "aib,aid->abd", leading_block_factor, d_first, preferred_element_type=jnp.float32
        )
        .astype(jnp.bfloat16)
        .reshape(tok_rows, feat_width)
    )
    grad_first = jnp.einsum(
        "aid,abd->aib", d_first, convolution_block_list, preferred_element_type=jnp.float32
    )
    d_convw = d_conv.astype(jnp.float32)
    conv_part = jnp.stack(
        [
            jnp.sum(d_convw * pad_feat[:-2], axis=0),
            jnp.sum(d_convw * feat_wide, axis=0),
            jnp.sum(d_convw * pad_feat[2:], axis=0),
        ]
    )
    pad_grad = extend(d_conv).astype(jnp.float32)
    conv_back = (
        conv_weight[0] * pad_grad[2:] + conv_weight[1] * d_convw + conv_weight[2] * pad_grad[:-2]
    )
    gate_back = lax.dot_general(
        d_gate, whole_gate, (((1,), (1,)), ((), ())), preferred_element_type=jnp.float32
    )
    grad_tokens = (conv_back + gate_back).astype(jnp.bfloat16)
    weight_part = lax.psum_scatter(
        lax.dot_general(
            features, d_gate, (((0,), (0,)), ((), ())), preferred_element_type=jnp.float32
        ),
        "seq",
        scatter_dimension=0,
        tiled=True,
    )
    grad_first, trailing_factor_gradient = lax.psum((grad_first, trailing_factor_gradient), "dp")
    grad_gate = lax.psum(weight_part, "dp")
    grad_conv = lax.psum(conv_part, ("seq", "dp"))
    return (
        mixed[None],
        grad_tokens[None],
        grad_conv,
        grad_gate,
        grad_first,
        trailing_factor_gradient,
    )


def solution(mesh):
    return jax.shard_map(
        shards,
        mesh=mesh,
        in_specs=(
            P("dp", "seq", None),
            P("dp", "seq", None),
            P(),
            P("seq", None),
            P("seq", None, None),
            P("seq", None, None),
        ),
        out_specs=(
            P("dp", "seq", None),
            P("dp", "seq", None),
            P(),
            P("seq", None),
            P("seq", None, None),
            P("seq", None, None),
        ),
        check_vma=False,
    )
```

profile of v0, /device:TPU:2, one launch (start us, length us, event | category | flops | bytes accessed | tf_op | source)
XLA Modules:
  0.0 599.1 jit_solution(1992488106284117112)
XLA Ops:
  7.9 68.7 %all-gather.2.cloned.1.call-done = bf16[1536,1536]{1,0:T(8,128)(2,1)} async-done(((bf16[48,1536]{1,0:T(8,128)(2,1)}), bf16[1536,1536]{1,0:T(8,128)(2,1)}) %all-gather.2.cloned.1.call-update) | async-done | bytes 4718608 | tf_op jit(solution)/shard_map/all_gather | solution.py:54
  76.6 7.6 %fusion.2 = (bf16[512,1536]{1,0:T(8,128)(2,1)S(1)}, f32[512,1536]{1,0:T(8,128)}) fusion(bf16[1,512,1536]{2,1,0:T(8,128)(2,1)} %param.7, bf16[1536,1536]{1,0:T(8,128)(2,1)} %all-gather.2.cloned.1.call-done, bf16[1,512,1536]{2,1,0:T(8,128)(2,1)} %param.6), kind=kOutput, calls=%fused_computation.9 | convolution fusion | flops 2418278400 | bytes 12582912 | tf_op jit(solution)/shard_map/dot_general | solution.py:55
  85.4 42.4 %all_to_all.63 = bf16[4,128,1536]{2,0,1:T(4,128)(2,1)S(1)} all-to-all(bf16[4,128,1536]{2,0,1:T(4,128)(2,1)S(1)} %copy.58), channel_id=1, replica_groups=mesh['seq'=32,'dp'=8] {'seq'}, dimensions={1} | all-to-all | bytes 3145728 | tf_op jit(solution)/shard_map/all_to_all | solution.py:61
  130.4 2.5 copy.61
  132.9 7.2 %all-to-all-start.3 = ((bf16[128,4,1536]{2,1,0:T(4,128)(2,1)}), bf16[128,4,1536]{2,1,0:T(4,128)(2,1)}, u32[]{:S(2)}, u32[]{:S(2)}) async-start(bf16[128,4,1536]{2,1,0:T(4,128)(2,1)} %copy.61), calls=%async_computation.3 | async-start | bytes 3145728 | tf_op jit(solution)/shard_map/all_to_all | solution.py:25
  140.9 2.1 collective-permute-start
  143.0 6.2 %collective-permute-start.1 = (bf16[1,1536]{1,0:T(2,128)(2,1)S(1)}, bf16[1,1536]{1,0:T(2,128)(2,1)S(1)}, u32[]{:S(2)}, u32[]{:S(2)}) collective-permute-start(bf16[1,1536]{1,0:T(2,128)(2,1)S(1)} %get-tuple-element.42), channel_id=1, source_target_pairs={{8,0},{16,8},{24,16},{32,24},{40,32},{48,40},{56,48},{64,56},{72,6... | collective-permute-start | bytes 9224 | tf_op jit(solution)/shard_map/ppermute | solution.py:15
  149.3 20.2 %collective-permute-done = bf16[1,1536]{1,0:T(2,128)(2,1)S(1)} collective-permute-done((bf16[1,1536]{1,0:T(2,128)(2,1)S(1)}, bf16[1,1536]{1,0:T(2,128)(2,1)S(1)}, u32[]{:S(2)}, u32[]{:S(2)}) %collective-permute-start) | collective-permute-done | bytes 3104 | tf_op jit(solution)/shard_map/ppermute | solution.py:14
  169.5 1.9 maximum_convert_fusion
  171.4 5.5 all-to-all-done.3
  176.9 3.1 copy.62
  180.0 3.7 all_to_all.58
  183.7 2.6 fusion.9
  186.3 1.6 fusion.7
  191.1 43.9 %all_to_all.64 = bf16[128,4,1536]{2,1,0:T(4,128)(2,1)S(1)} all-to-all(bf16[128,4,1536]{2,1,0:T(4,128)(2,1)S(1)} %copy.53), channel_id=1, replica_groups=mesh['seq'=32,'dp'=8] {'seq'}, dimensions={0} | all-to-all | bytes 3145728 | tf_op jit(solution)/shard_map/all_to_all | solution.py:25
  239.2 42.8 %all_to_all.65 = bf16[128,4,1536]{2,1,0:T(4,128)(2,1)S(1)} all-to-all(bf16[128,4,1536]{2,1,0:T(4,128)(2,1)S(1)} %copy.56), channel_id=1, replica_groups=mesh['seq'=32,'dp'=8] {'seq'}, dimensions={0} | all-to-all | bytes 3145728 | tf_op jit(solution)/shard_map/all_to_all | solution.py:25
  282.7 2.3 reshape.55
  284.9 9.1 %convolution_bitcast_fusion = f32[1536,1536]{0,1:T(8,128)} fusion(f32[1,512,1536]{2,1,0:T(8,128)} %reshape.55, bf16[1,512,1536]{2,1,0:T(8,128)(2,1)} %param.7, bf16[1,512,1536]{2,1,0:T(8,128)(2,1)} %param.6), kind=kOutput, calls=%fused_computation | convolution fusion | flops 2418278400 | bytes 15728640 | tf_op jit(solution)/shard_map/dot_general | solution.py:105
  294.1 9.6 %copy.70 = f32[1536,1536]{1,0:T(8,128)} copy(f32[1536,1536]{0,1:T(8,128)} %convolution_bitcast_fusion) | data formatting | bytes 18874368
  304.6 3.6 collective-permute-start.2
  308.2 4.7 collective-permute-start.3
  312.9 3.2 fusion.28
  316.1 75.9 %psum.28 = f32[3,1536]{1,0:T(4,128)} all-reduce(f32[3,1536]{1,0:T(4,128)S(1)} %pad_maximum_fusion), channel_id=1, replica_groups=mesh['seq'=32,'dp'=8] {'seq','dp'}, use_global_device_ids=true, to_apply=%region_3.0 | all-reduce | flops 4608 | bytes 36864 | tf_op jit(solution)/shard_map/psum | solution.py:114
  392.0 3.7 maximum_convert_fusion.1
  397.0 2.2 reshape.52
  399.3 50.2 %reduce-scatter.4.cloned.1.call-done = f32[48,1536]{1,0:T(8,128)} async-done(((f32[1536,1536]{1,0:T(8,128)}), f32[48,1536]{1,0:T(8,128)}) %reduce-scatter.4.cloned.1.call-update) | async-done | bytes 294928
  449.5 2.2 copy.71
  451.7 9.8 %fusion.14 = bf16[1,512,1536]{2,1,0:T(8,128)(2,1)} fusion(bf16[1536,1536]{1,0:T(8,128)(2,1)} %all-gather.2.cloned.1.call-done, f32[514,1536]{1,0:T(8,128)} %maximum_convert_fusion.1, bf16[512,1536]{1,0:T(8,128)(2,1)S(1)} %bitcast.78, f32[512,1536]{1,0:T(8,128)} %reshape.52, bf16[1,512,1536]{2,1,0:T(8,128)(2,1)} %param.7, f32[1536]{0:T(1024)S(1)} %get-tuple-element.33, ...), kind=kOutput, calls=%fused_computation.31 | convolution fusion | flops 2424569856 | bytes 18892800 | tf_op jit(solution)/shard_map/dot_general | solution.py:100
  461.5 1.6 fusion.15
  463.0 125.0 %all-reduce.3.cloned.1.call-done = (f32[48,1536]{0,1:T(8,128)}, f32[4,128,128]{2,1,0:T(8,128)}, f32[4,128,128]{2,1,0:T(8,128)}) async-done(((f32[48,1536]{0,1:T(8,128)}, f32[4,128,128]{2,1,0:T(8,128)}, f32[4,128,128]{2,1,0:T(8,128)}), (f32[48,1536]{0,1:T(8,128)}, f32[4,128,128]{2,1,0:T(8,128)}, f32[4,128,128]{2,1,0:T(8,128)})) %all-reduce.3.cloned.1.call-update) | async-done | bytes 819216 | tf_op jit(solution)/shard_map/psum | solution.py:113
  588.0 2.1 copy.67
  590.2 1.7 copy.83
  (58 shorter events, 16.4 us)
Async XLA Ops:
  7.2 176.5 %copy-start = (bf16[4,128,128]{2,1,0:T(8,128)(2,1)S(1)}, bf16[4,128,128]{2,1,0:T(8,128)(2,1)}, u32[]{:S(2)}) copy-start(bf16[4,128,128]{2,1,0:T(8,128)(2,1)} %param.10) | copy-start | bytes 393220
  7.2 69.4 %all-gather.2.cloned.1.call-start = ((), (), s32[]{:S(2)}) async-start(), calls=%async_computation.5 | async-start | bytes 4866048 | tf_op jit(solution)/shard_map/all_gather | solution.py:54
  127.8 1.9 copy-start.12
  128.5 1.1 copy-start.7
  132.9 16.3 %copy-start.14 = (f32[3,1536]{1,0:T(4,128)S(1)}, f32[3,1536]{1,0:T(4,128)}, u32[]{:S(2)}) copy-start(f32[3,1536]{1,0:T(4,128)} %param.8) | copy-start | bytes 55300
  132.9 44.0 %all-to-all-start.3 = ((bf16[128,4,1536]{2,1,0:T(4,128)(2,1)}), bf16[128,4,1536]{2,1,0:T(4,128)(2,1)}, u32[]{:S(2)}, u32[]{:S(2)}) async-start(bf16[128,4,1536]{2,1,0:T(4,128)(2,1)} %copy.61), calls=%async_computation.3 | async-start | bytes 3145728 | tf_op jit(solution)/shard_map/all_to_all | solution.py:25
  140.1 309.4 %reduce-scatter.4.cloned.1.call-start = ((), (), s32[]{:S(2)}) async-start(), calls=%async_computation.6 | async-start | bytes 9732096
  140.9 28.6 %collective-permute-start = (bf16[1,1536]{1,0:T(2,128)(2,1)S(1)}, bf16[1,1536]{1,0:T(2,128)(2,1)S(1)}, u32[]{:S(2)}, u32[]{:S(2)}) collective-permute-start(bf16[1,1536]{1,0:T(2,128)(2,1)S(1)} %get-tuple-element.41), channel_id=1, source_target_pairs={{0,8},{8,16},{16,24},{24,32},{32,40},{40,48},{48,56},{56,64},{64,7... | collective-permute-start | bytes 9224 | tf_op jit(solution)/shard_map/ppermute | solution.py:14
  143.0 26.5 %collective-permute-start.1 = (bf16[1,1536]{1,0:T(2,128)(2,1)S(1)}, bf16[1,1536]{1,0:T(2,128)(2,1)S(1)}, u32[]{:S(2)}, u32[]{:S(2)}) collective-permute-start(bf16[1,1536]{1,0:T(2,128)(2,1)S(1)} %get-tuple-element.42), channel_id=1, source_target_pairs={{8,0},{16,8},{24,16},{32,24},{40,32},{48,40},{56,48},{64,56},{72,6... | collective-permute-start | bytes 9224 | tf_op jit(solution)/shard_map/ppermute | solution.py:15
  183.7 2.6 copy-start.2
  186.3 1.6 copy-start.3
  187.9 1.2 copy-start.5
  235.8 1.2 copy-start.9
  303.8 284.3 %all-reduce.3.cloned.1.call-start = ((), (), s32[]{:S(2)}) async-start(), calls=%async_computation.7 | async-start | bytes 2621440 | tf_op jit(solution)/shard_map/psum | solution.py:113
  304.6 87.4 %collective-permute-start.2 = (bf16[1,1536]{1,0:T(2,128)(2,1)S(1)}, bf16[1,1536]{1,0:T(2,128)(2,1)S(1)}, u32[]{:S(2)}, u32[]{:S(2)}) collective-permute-start(bf16[1,1536]{1,0:T(2,128)(2,1)S(1)} %get-tuple-element.39), channel_id=1, source_target_pairs={{0,8},{8,16},{16,24},{24,32},{32,40},{40,48},{48,56},{56,64},{64,7... | collective-permute-start | bytes 9224 | tf_op jit(solution)/shard_map/ppermute | solution.py:14
  308.2 83.8 %collective-permute-start.3 = (bf16[1,1536]{1,0:T(2,128)(2,1)S(1)}, bf16[1,1536]{1,0:T(2,128)(2,1)S(1)}, u32[]{:S(2)}, u32[]{:S(2)}) collective-permute-start(bf16[1,1536]{1,0:T(2,128)(2,1)S(1)} %get-tuple-element.40), channel_id=1, source_target_pairs={{8,0},{16,8},{24,16},{32,24},{40,32},{48,40},{56,48},{64,56},{72,6... | collective-permute-start | bytes 9224 | tf_op jit(solution)/shard_map/ppermute | solution.py:15
  392.0 3.8 copy-start.8
  392.0 3.8 copy-start.10
  399.3 52.4 %copy-start.4 = (bf16[4,1536,128]{1,2,0:T(8,128)(2,1)S(1)}, bf16[4,1536,128]{1,2,0:T(8,128)(2,1)}, u32[]{:S(2)}) copy-start(bf16[4,1536,128]{1,2,0:T(8,128)(2,1)} %copy-done.3) | copy-start | bytes 4718596
  451.6 9.8 %copy-start.6 = (f32[512,1536]{1,0:T(8,128)S(1)}, f32[512,1536]{1,0:T(8,128)}, u32[]{:S(2)}) copy-start(f32[512,1536]{1,0:T(8,128)} %reshape.52) | copy-start | bytes 9437188
  451.7 9.8 %copy-start.11 = (f32[512,1536]{1,0:T(8,128)S(1)}, f32[512,1536]{1,0:T(8,128)}, u32[]{:S(2)}) copy-start(f32[512,1536]{1,0:T(8,128)} %get-tuple-element.44) | copy-start | bytes 9437188
  461.5 131.1 %copy-start.1 = (bf16[4,128,128]{2,1,0:T(8,128)(2,1)S(1)}, bf16[4,128,128]{2,1,0:T(8,128)(2,1)}, u32[]{:S(2)}) copy-start(bf16[4,128,128]{2,1,0:T(8,128)(2,1)} %param.10) | copy-start | bytes 393220
  588.0 3.8 copy-start.13
Sparse Core Ops, SparseCore 0:
  9.9 66.6 all-gather.1
  303.9 145.5 reduce-scatter.3
  452.9 135.0 all-reduce.2
where the time goes:
time: 600 us; the launch traced here: 599 us
  waiting for transfers between devices  270 us (45%)
  blocking collectives  205 us (34%)
  local copies, waits for them, and re-layouts  41 us (7%)
  matrix products  35.8 us (6%)
  starting transfers between devices  23.9 us (4%)
  between operations  14 us (2%)
  other arithmetic  9.23 us (2%)
    psum x1, waiting for transfers between devices, shards(): grad_gate = lax.psum(weight_part, 'dp')  125 us
    all_to_all x2, blocking collectives, regroup(): lax.all_to_all(values, 'seq', split_axis=0, concat_axis=1, tiled=True)  86.7 us
    psum x1, blocking collectives, shards(): grad_conv = lax.psum(conv_part, ('seq', 'dp'))  75.9 us
    all_gather x1, waiting for transfers between devices, shards(): whole_gate = lax.all_gather(gate_weight, 'seq', axis=0, tiled=True)  68.7 us
    unnamed x4, waiting for transfers between devices  50.9 us
    all_to_all x1, blocking collectives, shards(): lax.all_to_all(d_monarch.reshape(local_blocks, block_size, feat_width), '...  42.4 us
    ppermute x2, waiting for transfers between devices, with_halo(): before = lax.ppermute(last, axis, up)  20.2 us
    unnamed x35, local copies, waits for them, and re-layouts  19.9 us
  transfers between devices with their start and end apart: 8, of which 5 were waited for; matrix products, arithmetic and copies ran while one was open for 4% of the time, Pallas kernels for 0%

commit v1 on v0

--- a/solution.py
+++ b/solution.py
@@ -111,7 +111,7 @@
     )
     grad_first, trailing_factor_gradient = lax.psum((grad_first, trailing_factor_gradient), "dp")
     grad_gate = lax.psum(weight_part, "dp")
-    grad_conv = lax.psum(conv_part, ("seq", "dp"))
+    grad_conv = jnp.sum(lax.all_gather(conv_part, ("seq", "dp")), axis=0)
     return (
         mixed[None],
         grad_tokens[None],

time: 600 us -> 1320 us (2.20)
  waiting for transfers between devices: 270 us -> 1060 us
  blocking collectives: 205 us -> 129 us
    all_gather x0 -> x1, waiting for transfers between devices: none -> 717 us  [shards(): grad_conv = jnp.sum(lax.all_gather(conv_part, ('seq', 'dp')), axis=0)]
    psum x1 -> x0, blocking collectives: 75.9 us -> none  [shards(): grad_conv = lax.psum(conv_part, ('seq', 'dp'))]
    unnamed x4 -> x5, waiting for transfers between devices: 50.9 us -> 127 us
  transfers between devices with their start and end apart: 8 -> 9, of which waited for: 5 -> 6; matrix products, arithmetic and copies ran while one was open for 4% -> 2% of each run, Pallas kernels for 0% -> 0%
where the time goes in v1:
time: 1320 us
  waiting for transfers between devices  1060 us (80%)
  blocking collectives  129 us (10%)
  local copies, waits for them, and re-layouts  41.7 us (3%)
  matrix products  36 us (3%)
  starting transfers between devices  24.2 us (2%)
  between operations  14.1 us (1%)
    all_gather x1, waiting for transfers between devices, shards(): grad_conv = jnp.sum(lax.all_gather(conv_part, ('seq', 'dp')), axis=0)  717 us
    unnamed x5, waiting for transfers between devices  127 us
    psum x1, waiting for transfers between devices, shards(): grad_gate = lax.psum(weight_part, 'dp')  120 us
    all_to_all x2, blocking collectives, regroup(): lax.all_to_all(values, 'seq', split_axis=0, concat_axis=1, tiled=True)  86.7 us
    all_gather x1, waiting for transfers between devices, shards(): whole_gate = lax.all_gather(gate_weight, 'seq', axis=0, tiled=True)  68.7 us
    all_to_all x1, blocking collectives, shards(): lax.all_to_all(d_monarch.reshape(local_blocks, block_size, feat_width), '...  42.4 us
  transfers between devices with their start and end apart: 9, of which 6 were waited for; matrix products, arithmetic and copies ran while one was open for 2% of the time, Pallas kernels for 0%

profile of v1, /device:TPU:2, one launch (start us, length us, event | category | flops | bytes accessed | tf_op | source)
XLA Modules:
  0.0 1315.4 jit_solution(11920066574276222416)
XLA Ops:
  7.9 68.7 %all-gather.5.cloned.1.call-done = bf16[1536,1536]{1,0:T(8,128)(2,1)} async-done(((bf16[48,1536]{1,0:T(8,128)(2,1)}), bf16[1536,1536]{1,0:T(8,128)(2,1)}) %all-gather.5.cloned.1.call-update) | async-done | bytes 4718608 | tf_op jit(solution)/shard_map/all_gather | solution.py:54
  76.6 7.6 fusion.2
  85.4 42.4 %all_to_all.63 = bf16[4,128,1536]{2,0,1:T(4,128)(2,1)S(1)} all-to-all(bf16[4,128,1536]{2,0,1:T(4,128)(2,1)S(1)} %copy.58), channel_id=1, replica_groups=mesh['seq'=32,'dp'=8] {'seq'}, dimensions={1} | all-to-all | bytes 3145728 | tf_op jit(solution)/shard_map/all_to_all | solution.py:61
  130.5 2.5 copy.61
  132.9 7.2 all-to-all-start.3
  141.0 2.1 collective-permute-start
  143.0 6.2 collective-permute-start.1
  149.3 20.2 %collective-permute-done = bf16[1,1536]{1,0:T(2,128)(2,1)S(1)} collective-permute-done((bf16[1,1536]{1,0:T(2,128)(2,1)S(1)}, bf16[1,1536]{1,0:T(2,128)(2,1)S(1)}, u32[]{:S(2)}, u32[]{:S(2)}) %collective-permute-start) | collective-permute-done | bytes 3104 | tf_op jit(solution)/shard_map/ppermute | solution.py:14
  169.6 1.9 maximum_convert_fusion
  171.5 5.5 all-to-all-done.3
  176.9 3.1 copy.62
  180.0 3.7 all_to_all.58
  183.7 2.6 fusion.9
  191.2 43.9 %all_to_all.64 = bf16[128,4,1536]{2,1,0:T(4,128)(2,1)S(1)} all-to-all(bf16[128,4,1536]{2,1,0:T(4,128)(2,1)S(1)} %copy.53), channel_id=1, replica_groups=mesh['seq'=32,'dp'=8] {'seq'}, dimensions={0} | all-to-all | bytes 3145728 | tf_op jit(solution)/shard_map/all_to_all | solution.py:25
  239.1 42.8 %all_to_all.65 = bf16[128,4,1536]{2,1,0:T(4,128)(2,1)S(1)} all-to-all(bf16[128,4,1536]{2,1,0:T(4,128)(2,1)S(1)} %copy.56), channel_id=1, replica_groups=mesh['seq'=32,'dp'=8] {'seq'}, dimensions={0} | all-to-all | bytes 3145728 | tf_op jit(solution)/shard_map/all_to_all | solution.py:25
  282.7 2.3 reshape.55
  285.0 9.1 convolution_bitcast_fusion
  294.1 9.6 copy.70
  305.4 3.6 collective-permute-start.2
  309.0 5.0 collective-permute-start.3
  314.0 3.3 fusion.28
  317.4 2.2 maximum_convert_fusion.1
  321.6 2.3 reshape.52
  323.9 126.0 %reduce-scatter.4.cloned.1.call-done = f32[48,1536]{1,0:T(8,128)} async-done(((f32[1536,1536]{1,0:T(8,128)}), f32[48,1536]{1,0:T(8,128)}) %reduce-scatter.4.cloned.1.call-update) | async-done | bytes 294928
  449.9 2.1 copy.71
  452.1 9.8 fusion.14
  461.9 1.6 fusion.15
  463.4 716.7 %all-gather.7.cloned.1.call-done = f32[256,3,1536]{2,1,0:T(4,128)} async-done(((f32[1,3,1536]{2,1,0:T(4,128)}), f32[256,3,1536]{2,1,0:T(4,128)}) %all-gather.7.cloned.1.call-update) | async-done | bytes 4718608 | tf_op jit(solution)/shard_map/all_gather | solution.py:114
  1180.1 4.3 reduce_sum.39
  1184.5 119.8 %all-reduce.3.cloned.1.call-done = (f32[48,1536]{0,1:T(8,128)}, f32[4,128,128]{2,1,0:T(8,128)}, f32[4,128,128]{2,1,0:T(8,128)}) async-done(((f32[48,1536]{0,1:T(8,128)}, f32[4,128,128]{2,1,0:T(8,128)}, f32[4,128,128]{2,1,0:T(8,128)}), (f32[48,1536]{0,1:T(8,128)}, f32[4,128,128]{2,1,0:T(8,128)}, f32[4,128,128]{2,1,0:T(8,128)})) %all-reduce.3.cloned.1.call-update) | async-done | bytes 819216 | tf_op jit(solution)/shard_map/psum | solution.py:113
  1304.3 2.1 copy.67
  1306.4 1.7 copy.83
  (63 shorter events, 19.3 us)
Async XLA Ops:
  7.2 176.6 %copy-start = (bf16[4,128,128]{2,1,0:T(8,128)(2,1)S(1)}, bf16[4,128,128]{2,1,0:T(8,128)(2,1)}, u32[]{:S(2)}) copy-start(bf16[4,128,128]{2,1,0:T(8,128)(2,1)} %param.10) | copy-start | bytes 393220
  7.2 69.4 %all-gather.5.cloned.1.call-start = ((), (), s32[]{:S(2)}) async-start(), calls=%async_computation.5 | async-start | bytes 4866048 | tf_op jit(solution)/shard_map/all_gather | solution.py:54
  127.8 1.9 copy-start.13
  128.6 1.1 copy-start.8
  132.9 16.3 %copy-start.15 = (f32[3,1536]{1,0:T(4,128)S(1)}, f32[3,1536]{1,0:T(4,128)}, u32[]{:S(2)}) copy-start(f32[3,1536]{1,0:T(4,128)} %param.8) | copy-start | bytes 55300
  132.9 44.0 %all-to-all-start.3 = ((bf16[128,4,1536]{2,1,0:T(4,128)(2,1)}), bf16[128,4,1536]{2,1,0:T(4,128)(2,1)}, u32[]{:S(2)}, u32[]{:S(2)}) async-start(bf16[128,4,1536]{2,1,0:T(4,128)(2,1)} %copy.61), calls=%async_computation.3 | async-start | bytes 3145728 | tf_op jit(solution)/shard_map/all_to_all | solution.py:25
  140.1 309.7 %reduce-scatter.4.cloned.1.call-start = ((), (), s32[]{:S(2)}) async-start(), calls=%async_computation.7 | async-start | bytes 9732096
  141.0 28.6 %collective-permute-start = (bf16[1,1536]{1,0:T(2,128)(2,1)S(1)}, bf16[1,1536]{1,0:T(2,128)(2,1)S(1)}, u32[]{:S(2)}, u32[]{:S(2)}) collective-permute-start(bf16[1,1536]{1,0:T(2,128)(2,1)S(1)} %get-tuple-element.41), channel_id=1, source_target_pairs={{0,8},{8,16},{16,24},{24,32},{32,40},{40,48},{48,56},{56,64},{64,7... | collective-permute-start | bytes 9224 | tf_op jit(solution)/shard_map/ppermute | solution.py:14
  143.0 26.5 %collective-permute-start.1 = (bf16[1,1536]{1,0:T(2,128)(2,1)S(1)}, bf16[1,1536]{1,0:T(2,128)(2,1)S(1)}, u32[]{:S(2)}, u32[]{:S(2)}) collective-permute-start(bf16[1,1536]{1,0:T(2,128)(2,1)S(1)} %get-tuple-element.42), channel_id=1, source_target_pairs={{8,0},{16,8},{24,16},{32,24},{40,32},{48,40},{56,48},{64,56},{72,6... | collective-permute-start | bytes 9224 | tf_op jit(solution)/shard_map/ppermute | solution.py:15
  183.7 2.6 copy-start.2
  186.3 1.6 copy-start.3
  187.9 1.2 copy-start.6
  235.9 1.2 copy-start.10
  303.8 876.3 %all-gather.7.cloned.1.call-start = ((), (), s32[]{:S(2)}) async-start(), calls=%async_computation.6 | async-start | bytes 6316032 | tf_op jit(solution)/shard_map/all_gather | solution.py:114
  304.5 999.8 %all-reduce.3.cloned.1.call-start = ((), (), s32[]{:S(2)}) async-start(), calls=%async_computation.8 | async-start | bytes 2621440 | tf_op jit(solution)/shard_map/psum | solution.py:113
  305.4 12.0 collective-permute-start.2
  309.0 8.4 copy-start.4
  309.0 8.4 collective-permute-start.3
  317.4 2.2 copy-start.9
  317.4 2.9 copy-start.11
  323.9 128.2 %copy-start.5 = (bf16[4,1536,128]{1,2,0:T(8,128)(2,1)S(1)}, bf16[4,1536,128]{1,2,0:T(8,128)(2,1)}, u32[]{:S(2)}) copy-start(bf16[4,1536,128]{1,2,0:T(8,128)(2,1)} %copy-done.3) | copy-start | bytes 4718596
  452.1 9.8 copy-start.7
  452.1 9.8 copy-start.12
  1180.1 128.7 %copy-start.1 = (bf16[4,128,128]{2,1,0:T(8,128)(2,1)S(1)}, bf16[4,128,128]{2,1,0:T(8,128)(2,1)}, u32[]{:S(2)}) copy-start(bf16[4,128,128]{2,1,0:T(8,128)(2,1)} %param.10) | copy-start | bytes 393220
  1304.3 3.8 copy-start.14
Sparse Core Ops, SparseCore 0:
  9.9 66.6 all-gather.4
  303.9 145.9 reduce-scatter.3
  452.3 727.7 all-gather.6
  1183.4 120.8 all-reduce.2
